TPU v7x, 512 devices: a whole 4x4x16 slice. The times are simulated.
512 devices in a mesh: pair: 128 (over z, x, core), red: 4 (over y).
Axes of the slice: x: 4, y: 4, z: 16, core: 2. Of those that a mesh axis runs over, the one named last changes fastest.
Arguments:
- amplitudes: bfloat16 [256, 128, 1024], P('pair', None, 'red'), may hold values from -6 to 6
- ladder_ints: bfloat16 [128, 1024, 1024], P('pair', 'red'), may hold values from -0.25 to 0.25
- live_count: int32 [128], replicated, may hold values from 128 to 1024, as said below
Outputs:
- residual: bfloat16 [256, 128, 1024], P('pair', None, 'red')
Inputs may be any that keep to these rules, and one draw needn't show every extreme that they name: Only contracted pairs c < live_count[s] of slab s take part; in every draw some slab has all 1024 pairs live.
All inputs are finite; a program needn't handle non-finite values.
Results may differ from a plain program's by a relative error of at most 0.012.
Values may be sent and summed in bfloat16 or wider, within the bound.
A program may use at most 128 MiB of HBM per device.

v0:
```python
import jax
import jax.numpy as jnp
from jax import lax
from jax.sharding import PartitionSpec as P


def reduce_shares(partial_value):
    share_width = partial_value.shape[2] // lax.axis_size("red")
    summed = lax.psum(partial_value.astype(jnp.bfloat16), "red").astype(jnp.float32)
    return lax.dynamic_slice_in_dim(summed, lax.axis_index("red") * share_width, share_width, 2)


def body(amplitudes, ladder_ints, live_count):
    slab_index = lax.axis_index("pair")
    share_index = lax.axis_index("red")
    regrouped = lax.all_to_all(amplitudes, "pair", split_axis=1, concat_axis=0, tiled=True)
    block = regrouped[:, 0, :]
    share_width = block.shape[1]
    slab_count = live_count.shape[0]
    live_limit = jnp.sum(
        jnp.where(jnp.arange(slab_count, dtype=jnp.int32) == slab_index, live_count, 0)
    )
    position = share_index * share_width + jnp.arange(share_width, dtype=jnp.int32)
    masked = jnp.where(position[None, :] < live_limit, block, jnp.zeros_like(block))
    partial_value = jnp.dot(masked, ladder_ints[0], preferred_element_type=jnp.float32)
    partial_value = partial_value[:, None, :]
    moved = lax.all_to_all(
        partial_value.astype(jnp.bfloat16), "pair", split_axis=0, concat_axis=1, tiled=True
    )
    return reduce_shares(moved.astype(jnp.float32)).astype(jnp.bfloat16)


def solution(mesh):
    in_specs = (P("pair", None, "red"), P("pair", "red", None), P())
    out_specs = P("pair", None, "red")
    return jax.shard_map(body, mesh=mesh, in_specs=in_specs, out_specs=out_specs, check_vma=False)
```

profile of v0, /device:TPU:1, one launch (start us, length us, event | category | flops | bytes accessed | tf_op | source)
XLA Modules:
  0.0 148.3 jit_solution(17337359764642066357)
XLA Ops:
  6.5 0.0 copy-start
  6.5 1.8 %copy.10 = bf16[2,128,256]{2,0,1:T(2,128)(2,1)} copy(bf16[2,128,256]{2,1,0:T(8,128)(2,1)} %param.3) | data formatting | bytes 262144 | tf_op args[0]
  8.3 20.4 %all-to-all-start = ((bf16[2,128,256]{2,0,1:T(2,128)(2,1)}), bf16[2,128,256]{2,0,1:T(2,128)(2,1)S(1)}, u32[]{:S(2)}, u32[]{:S(2)}) async-start(bf16[2,128,256]{2,0,1:T(2,128)(2,1)} %copy.10), calls=%async_computation | async-start | bytes 262144 | tf_op jit(solution)/shard_map/all_to_all | solution.py:16
  28.7 0.0 all-reduce.2.cloned.1.call-start
  28.7 0.0 copy-start.1
  28.8 0.6 copy-done.1
  29.4 0.7 fusion.3
  30.1 0.7 add_compare_fusion
  30.8 13.9 %all-to-all-done = bf16[2,128,256]{2,0,1:T(2,128)(2,1)S(1)} async-done(((bf16[2,128,256]{2,0,1:T(2,128)(2,1)}), bf16[2,128,256]{2,0,1:T(2,128)(2,1)S(1)}, u32[]{:S(2)}, u32[]{:S(2)}) %all-to-all-start) | async-done | bytes 131104 | tf_op jit(solution)/shard_map/all_to_all | solution.py:16
  44.8 0.1 fusion.2
  44.9 0.1 select_n.20
  44.9 0.0 copy-done
  44.9 0.3 fusion
  45.2 0.5 broadcast.20
  45.8 1.0 reduce.1
  46.8 0.2 reshape.16
  47.0 37.8 %all_to_all.30 = bf16[128,2,1024]{2,1,0:T(2,128)(2,1)S(1)} all-to-all(bf16[128,2,1024]{2,1,0:T(2,128)(2,1)S(1)} %reshape.16), channel_id=1, replica_groups=mesh['pair'=128,'red'=4] {'pair'}, dimensions={0} | all-to-all | bytes 1048576 | tf_op jit(solution)/shard_map/all_to_all | solution.py:27
  84.8 0.4 reshape.17
  85.2 3.1 %reduce = bf16[256,1024]{1,0:T(8,128)(2,1)S(1)} reduce(bf16[256,1,1024]{2,1,0:T(2,128)(2,1)S(1)} %reshape.17, bf16[]{:T(256)} %constant.19), dimensions={1}, to_apply=%all_to_all.24.reduce_sub_computation | reduce | bytes 1048578 | tf_op jit(solution)/shard_map/all_to_all | solution.py:27
  88.3 1.0 all_to_all.25
  89.3 0.0 all-reduce.2.cloned.1.call-update
  89.3 50.5 %all-reduce.2.cloned.1.call-done = bf16[2,128,1024]{2,0,1:T(2,128)(2,1)} async-done(((bf16[2,128,1024]{2,0,1:T(2,128)(2,1)}), bf16[2,128,1024]{2,0,1:T(2,128)(2,1)}) %all-reduce.2.cloned.1.call-update) | async-done | bytes 524304 | tf_op jit(solution)/shard_map/psum | solution.py:9
  139.8 1.0 convert_convert_fusion
  140.8 0.7 copy.12
Async XLA Ops:
  6.5 38.4 %copy-start = (bf16[1,256,1024]{2,1,0:T(8,128)(2,1)S(1)}, bf16[1,256,1024]{2,1,0:T(8,128)(2,1)}, u32[]{:S(2)}) copy-start(bf16[1,256,1024]{2,1,0:T(8,128)(2,1)} %param.4) | copy-start | bytes 1572868
  8.3 36.5 %all-to-all-start = ((bf16[2,128,256]{2,0,1:T(2,128)(2,1)}), bf16[2,128,256]{2,0,1:T(2,128)(2,1)S(1)}, u32[]{:S(2)}, u32[]{:S(2)}) async-start(bf16[2,128,256]{2,0,1:T(2,128)(2,1)} %copy.10), calls=%async_computation | async-start | bytes 262144 | tf_op jit(solution)/shard_map/all_to_all | solution.py:16
  28.7 111.1 %all-reduce.2.cloned.1.call-start = ((), (), s32[]{:S(2)}) async-start(), calls=%async_computation.2 | async-start | bytes 1048576 | tf_op jit(solution)/shard_map/psum | solution.py:9
  28.7 0.7 copy-start.1
Sparse Core Ops, SparseCore 0:
  89.4 50.3 all-reduce.1
where the time goes:
time: 150 us; the launch traced here: 148 us
  waiting for transfers between devices  64.4 us (43%)
  blocking collectives  37.8 us (25%)
  starting transfers between devices  20.4 us (14%)
  between operations  13.5 us (9%)
  other arithmetic  6.59 us (4%)
  local copies, waits for them, and re-layouts  5.29 us (4%)
    psum x1, waiting for transfers between devices, reduce_shares(): lax.psum(partial_value.astype(jnp.bfloat16), 'red').astype(jnp.float32)  50.5 us
    all_to_all x1, blocking collectives, body(): lax.all_to_all(partial_value.astype(jnp.bfloat16), 'pair', split_axis=0,...  37.8 us
    all_to_all x1, starting transfers between devices, body(): lax.all_to_all(amplitudes, 'pair', split_axis=1, concat_axis=0, tiled=True)  20.4 us
    all_to_all x1, waiting for transfers between devices, body(): lax.all_to_all(amplitudes, 'pair', split_axis=1, concat_axis=0, tiled=True)  13.9 us
    all_to_all x1, other arithmetic, body(): lax.all_to_all(partial_value.astype(jnp.bfloat16), 'pair', split_axis=0,...  3.05 us
    unnamed x7, local copies, waits for them, and re-layouts  3.04 us
  transfers between devices with their start and end apart: 2, of which 2 were waited for; matrix products, arithmetic and copies ran while one was open for 1% of the time, Pallas kernels for 0%

commit v1 on v0

v1 whole, which is shorter than its diff:
```python
import functools

import jax
import jax.numpy as jnp
from jax import lax
from jax.experimental import pallas as pl
from jax.experimental.pallas import tpu as pltpu
from jax.sharding import PartitionSpec as P

MESH = pl.DeviceIdType.MESH
NZ = 16
NX = 8
NR = 4
PLANES = 2
CHUNKS = NZ // PLANES
FAR = [8] + [d for i in range(7, 0, -1) for d in (i, 16 - i)]


def kernel(amp_ref, w_ref, live_ref, out_ref, amp, w, live, xs, ra, rb, pb, rr, ob,
           lsem, asem, bsem, rsem, osem, asend, bsend, rsend, osend, ready):
    me = lax.axis_index("pair")
    r = lax.axis_index("red")
    z = me // NX
    xc = lax.rem(me, NX)

    barrier = pltpu.get_barrier_semaphore()
    for k in range(1, NZ):
        pl.semaphore_signal(barrier, inc=1, device_id=(lax.rem(z + k, NZ) * NX + xc, r), device_id_type=MESH)
    for k in range(1, NX):
        pl.semaphore_signal(barrier, inc=1, device_id=(z * NX + lax.rem(xc + k, NX), r), device_id_type=MESH)
    for k in range(1, NR):
        pl.semaphore_signal(barrier, inc=1, device_id=(me, lax.rem(r + k, NR)), device_id_type=MESH)

    loads = [pltpu.make_async_copy(amp_ref, amp, lsem.at[0]),
             pltpu.make_async_copy(w_ref, w, lsem.at[1]),
             pltpu.make_async_copy(live_ref, live, lsem.at[2])]
    for copy in loads:
        copy.start()
    loads[0].wait()
    xs[...] = jnp.stack([amp[0], amp[1]], axis=1).reshape(NZ, NX, 2, 256)
    loads[1].wait()
    loads[2].wait()
    limit = live[me] - r * 256
    rows = lax.broadcasted_iota(jnp.int32, (256, 1024), 0)
    w[0] = jnp.where(rows < limit, w[0], jnp.zeros_like(w[0]))

    pl.semaphore_wait(barrier, NZ + NX + NR - 3)
    for k in FAR:
        zz = lax.rem(z + k, NZ)
        pltpu.make_async_remote_copy(xs.at[zz], ra.at[z], asend, asem.at[z // PLANES],
                                     device_id=(zz * NX + xc, r), device_id_type=MESH).start()
    pltpu.make_async_copy(xs.at[z], ra.at[z], asem.at[z // PLANES]).start()
    for k in range(1, NX):
        pl.semaphore_signal(ready, inc=1, device_id=(z * NX + lax.rem(xc + k, NX), r), device_id_type=MESH)

    def forward(c):
        span = pl.ds(c * PLANES, PLANES)
        pltpu.make_async_copy(ra.at[span], ra.at[span], asem.at[c]).wait()
        for k in range(1, NX):
            q = lax.rem(xc + k, NX)
            pltpu.make_async_remote_copy(ra.at[span, q], rb.at[span, xc], bsend, bsem.at[c],
                                         device_id=(z * NX + q, r), device_id_type=MESH).start()
        pltpu.make_async_copy(ra.at[span, xc], rb.at[span, xc], bsem.at[c]).start()

    def multiply(c):
        span = pl.ds(c * PLANES, PLANES)
        pltpu.make_async_copy(rb.at[span], rb.at[span], bsem.at[c]).wait()
        rows = rb[span].reshape(PLANES * NX * 2, 256)
        part = jnp.dot(rows, w[0], preferred_element_type=jnp.float32).astype(jnp.bfloat16)
        for j in range(NR):
            pb[c, j] = part[:, j * 256:(j + 1) * 256]
        for k in (2, 1, 3):
            rk = lax.rem(r + k, NR)
            pltpu.make_async_remote_copy(pb.at[c, rk], rr.at[c, k - 1], rsend, rsem.at[c],
                                         device_id=(me, rk), device_id_type=MESH).start()

    def reduce(c):
        pltpu.make_async_copy(rr.at[c], rr.at[c], rsem.at[c]).wait()
        total = pb[c, r].astype(jnp.float32)
        for k in range(NR - 1):
            total = total + rr[c, k].astype(jnp.float32)
        ob[pl.ds(c * PLANES * NX, PLANES * NX)] = total.astype(jnp.bfloat16).reshape(PLANES * NX, 2, 256)

        def send(i, carry):
            p = c * PLANES * NX + i

            @pl.when(p != me)
            def _():
                pltpu.make_async_remote_copy(ob.at[p], out_ref.at[me], osend, osem,
                                             device_id=(p, r), device_id_type=MESH).start()

            @pl.when(p == me)
            def _():
                pltpu.make_async_copy(ob.at[p], out_ref.at[me], osem).start()

            return carry

        lax.fori_loop(0, PLANES * NX, send, 0)

    for t in range(CHUNKS + 2):
        if t < CHUNKS:
            forward(t)
        if 0 <= t - 1 < CHUNKS:
            multiply(t - 1)
        if t == 2:
            pl.semaphore_wait(ready, NX - 1)
        if 0 <= t - 2 < CHUNKS:
            reduce(t - 2)

    pltpu.make_async_copy(out_ref, out_ref, osem).wait()
    pltpu.make_async_copy(xs.at[pl.ds(0, NZ - 1)], xs.at[pl.ds(0, NZ - 1)], asend).wait()
    pltpu.make_async_copy(rb.at[:, pl.ds(0, NX - 1)], rb.at[:, pl.ds(0, NX - 1)], bsend).wait()
    pltpu.make_async_copy(rr, rr, rsend).wait()
    pltpu.make_async_copy(ob.at[pl.ds(0, NZ * NX - 1)], ob.at[pl.ds(0, NZ * NX - 1)], osend).wait()


def body(amplitudes, ladder_ints, live_count):
    any_space = pl.BlockSpec(memory_space=pl.ANY)
    bf16 = jnp.bfloat16
    out = pl.pallas_call(
        kernel,
        out_shape=jax.ShapeDtypeStruct((NZ * NX, 2, 256), bf16),
        in_specs=[any_space] * 3,
        out_specs=any_space,
        scratch_shapes=[
            pltpu.VMEM((2, 128, 256), bf16),
            pltpu.VMEM((1, 256, 1024), bf16),
            pltpu.SMEM((128,), jnp.int32),
            pltpu.VMEM((NZ, NX, 2, 256), bf16),
            pltpu.VMEM((NZ, NX, 2, 256), bf16),
            pltpu.VMEM((NZ, NX, 2, 256), bf16),
            pltpu.VMEM((CHUNKS, NR, PLANES * NX * 2, 256), bf16),
            pltpu.VMEM((CHUNKS, NR - 1, PLANES * NX * 2, 256), bf16),
            pltpu.VMEM((NZ * NX, 2, 256), bf16),
            pltpu.SemaphoreType.DMA((3,)),
            pltpu.SemaphoreType.DMA((CHUNKS,)),
            pltpu.SemaphoreType.DMA((CHUNKS,)),
            pltpu.SemaphoreType.DMA((CHUNKS,)),
            pltpu.SemaphoreType.DMA,
            pltpu.SemaphoreType.DMA,
            pltpu.SemaphoreType.DMA,
            pltpu.SemaphoreType.DMA,
            pltpu.SemaphoreType.DMA,
            pltpu.SemaphoreType.REGULAR,
        ],
        compiler_params=pltpu.CompilerParams(collective_id=0, has_side_effects=True),
    )(amplitudes, ladder_ints, live_count)
    return jnp.transpose(out, (1, 0, 2))


def solution(mesh):
    in_specs = (P("pair", None, "red"), P("pair", "red", None), P())
    out_specs = P("pair", None, "red")
    return jax.shard_map(body, mesh=mesh, in_specs=in_specs, out_specs=out_specs, check_vma=False)
```

time: 150 us -> 51.1 us (0.34)
  waiting for transfers between devices: 64.4 us -> 0 us
  Pallas kernels: 0 us -> 49.2 us
  blocking collectives: 37.8 us -> 0 us
  starting transfers between devices: 20.4 us -> 0 us
  between operations: 13.5 us -> 0.01 us
  other arithmetic: 6.59 us -> 0 us
  local copies, waits for them, and re-layouts: 5.29 us -> 1.57 us
    psum x1 -> x0, waiting for transfers between devices: 50.5 us -> none  [reduce_shares(): lax.psum(partial_value.astype(jnp.bfloat16), 'red').astype(jnp.float32)]
    pallas_call x0 -> x1, Pallas kernels: none -> 49.2 us  [body(): pl.pallas_call(kernel, out_shape=jax.ShapeDtypeStruct((NZ * NX, 2, 256),...]
    all_to_all x1 -> x0, blocking collectives: 37.8 us -> none  [body(): lax.all_to_all(partial_value.astype(jnp.bfloat16), 'pair', split_axis=0,...]
    all_to_all x1 -> x0, starting transfers between devices: 20.4 us -> none  [body(): lax.all_to_all(amplitudes, 'pair', split_axis=1, concat_axis=0, tiled=True)]
    all_to_all x1 -> x0, waiting for transfers between devices: 13.9 us -> none  [body(): lax.all_to_all(amplitudes, 'pair', split_axis=1, concat_axis=0, tiled=True)]
    all_to_all x1 -> x0, other arithmetic: 3.05 us -> none  [body(): lax.all_to_all(partial_value.astype(jnp.bfloat16), 'pair', split_axis=0,...]
    unnamed x7 -> x0, local copies, waits for them, and re-layouts: 3.04 us -> none
    convert_element_type x2 -> x0, other arithmetic: 2.03 us -> none  [the longest x1 1.03 us: body(): partial_value.astype(jnp.bfloat16)]
  transfers between devices with their start and end apart: 2 -> 0, of which waited for: 2 -> 0; matrix products, arithmetic and copies ran while one was open for 1% -> 0% of each run, Pallas kernels for 0% -> 0%
where the time goes in v1:
time: 51.1 us; the launch traced here: 50.7 us
  Pallas kernels  49.2 us (96%)
  local copies, waits for them, and re-layouts  1.57 us (3%)
    pallas_call x1, Pallas kernels, body(): pl.pallas_call(kernel, out_shape=jax.ShapeDtypeStruct((NZ * NX, 2, 256),...  49.2 us
    transpose x1, local copies, waits for them, and re-layouts, body(): return jnp.transpose(out, (1, 0, 2))  1.57 us

profile of v1, /device:TPU:1, one launch (start us, length us, event | category | flops | bytes accessed | tf_op | source)
XLA Modules:
  0.0 50.7 jit_solution(8528169152332891288)
XLA Ops:
  0.0 49.2 %shard_map.37 = bf16[128,2,256]{2,1,0:T(2,128)(2,1)} custom-call(bf16[2,128,256]{2,1,0:T(8,128)(2,1)} %amp_ref.1, bf16[1,256,1024]{2,1,0:T(8,128)(2,1)} %w_ref.1, s32[128]{0:T(128)} %live_ref.1), custom_call_target="tpu_custom_call" | custom-call | tf_op jit(solution)/shard_map/pallas_call | solution.py:120
  49.2 1.6 %copy.4 = bf16[2,128,256]{2,1,0:T(8,128)(2,1)} copy(bf16[2,128,256]{2,0,1:T(2,128)(2,1)} %bitcast.1) | data formatting | bytes 262144 | tf_op jit(solution)/shard_map/transpose | solution.py:148

commit v2 on v1

v2 whole, which is shorter than its diff:
```python
import jax
import jax.numpy as jnp
from jax import lax
from jax.experimental import pallas as pl
from jax.experimental.pallas import tpu as pltpu
from jax.sharding import PartitionSpec as P

MESH = pl.DeviceIdType.MESH
NZ = 16
NX = 8
NR = 4
PLANES = 2
CHUNKS = NZ // PLANES
LAG = 5
PAIRS = PLANES * NX
FAR = [8] + [d for i in range(7, 0, -1) for d in (i, 16 - i)]


def kernel(amp_ref, w_ref, live_ref, out_ref, amp, w, live, xs, rb, pb, rr, ob,
           lsem, bsem, rsem, osem, bsend, rsend, osend):
    me = lax.axis_index("pair")
    r = lax.axis_index("red")
    z = me // NX
    xc = lax.rem(me, NX)

    partners = [lax.rem(z + dz, NZ) * NX + lax.rem(xc + k, NX)
                for dz in FAR + [0] for k in range(NX) if (dz, k) != (0, 0)]

    barrier = pltpu.get_barrier_semaphore()
    for p in partners:
        pl.semaphore_signal(barrier, inc=1, device_id=(p, r), device_id_type=MESH)
    for k in range(1, NR):
        pl.semaphore_signal(barrier, inc=1, device_id=(me, lax.rem(r + k, NR)), device_id_type=MESH)

    loads = [pltpu.make_async_copy(amp_ref, amp, lsem.at[0]),
             pltpu.make_async_copy(w_ref, w, lsem.at[1]),
             pltpu.make_async_copy(live_ref, live, lsem.at[2])]
    for copy in loads:
        copy.start()
    loads[0].wait()
    xs[...] = jnp.stack([amp[0], amp[1]], axis=1)
    loads[1].wait()
    loads[2].wait()
    limit = live[me] - r * 256
    rows = lax.broadcasted_iota(jnp.int32, (256, 1024), 0)
    w[0] = jnp.where(rows < limit, w[0], jnp.zeros_like(w[0]))

    pl.semaphore_wait(barrier, NZ * NX - 1 + NR - 1)
    for p in partners:
        pltpu.make_async_remote_copy(xs.at[p], rb.at[me], bsend, bsem.at[z // PLANES],
                                     device_id=(p, r), device_id_type=MESH).start()
    pltpu.make_async_copy(xs.at[me], rb.at[me], bsem.at[z // PLANES]).start()

    def multiply(c):
        span = pl.ds(c * PAIRS, PAIRS)
        pltpu.make_async_copy(rb.at[span], rb.at[span], bsem.at[c]).wait()
        rows = rb[span].reshape(PAIRS * 2, 256)
        part = jnp.dot(rows, w[0], preferred_element_type=jnp.float32).astype(jnp.bfloat16)
        for j in range(NR):
            pb[c, j] = part[:, j * 256:(j + 1) * 256]
        for k in (2, 1, 3):
            rk = lax.rem(r + k, NR)
            pltpu.make_async_remote_copy(pb.at[c, rk], rr.at[c, k - 1], rsend, rsem.at[c],
                                         device_id=(me, rk), device_id_type=MESH).start()

    def reduce(c):
        pltpu.make_async_copy(rr.at[c], rr.at[c], rsem.at[c]).wait()
        total = pb[c, r].astype(jnp.float32)
        for k in range(NR - 1):
            total = total + rr[c, k].astype(jnp.float32)
        ob[pl.ds(c * PAIRS, PAIRS)] = total.astype(jnp.bfloat16).reshape(PAIRS, 2, 256)

        def send(i, carry):
            p = c * PAIRS + i

            @pl.when(p != me)
            def _():
                pltpu.make_async_remote_copy(ob.at[p], out_ref.at[me], osend, osem,
                                             device_id=(p, r), device_id_type=MESH).start()

            @pl.when(p == me)
            def _():
                pltpu.make_async_copy(ob.at[p], out_ref.at[me], osem).start()

            return carry

        lax.fori_loop(0, PAIRS, send, 0)

    for t in range(CHUNKS + LAG):
        if t < CHUNKS:
            multiply(t)
        if t >= LAG:
            reduce(t - LAG)

    pltpu.make_async_copy(out_ref, out_ref, osem).wait()
    pltpu.make_async_copy(xs.at[pl.ds(0, NZ * NX - 1)], xs.at[pl.ds(0, NZ * NX - 1)], bsend).wait()
    pltpu.make_async_copy(rr, rr, rsend).wait()
    pltpu.make_async_copy(ob.at[pl.ds(0, NZ * NX - 1)], ob.at[pl.ds(0, NZ * NX - 1)], osend).wait()


def body(amplitudes, ladder_ints, live_count):
    any_space = pl.BlockSpec(memory_space=pl.ANY)
    bf16 = jnp.bfloat16
    out = pl.pallas_call(
        kernel,
        out_shape=jax.ShapeDtypeStruct((NZ * NX, 2, 256), bf16),
        in_specs=[any_space] * 3,
        out_specs=any_space,
        scratch_shapes=[
            pltpu.VMEM((2, 128, 256), bf16),
            pltpu.VMEM((1, 256, 1024), bf16),
            pltpu.SMEM((128,), jnp.int32),
            pltpu.VMEM((NZ * NX, 2, 256), bf16),
            pltpu.VMEM((NZ * NX, 2, 256), bf16),
            pltpu.VMEM((CHUNKS, NR, PAIRS * 2, 256), bf16),
            pltpu.VMEM((CHUNKS, NR - 1, PAIRS * 2, 256), bf16),
            pltpu.VMEM((NZ * NX, 2, 256), bf16),
            pltpu.SemaphoreType.DMA((3,)),
            pltpu.SemaphoreType.DMA((CHUNKS,)),
            pltpu.SemaphoreType.DMA((CHUNKS,)),
            pltpu.SemaphoreType.DMA,
            pltpu.SemaphoreType.DMA,
            pltpu.SemaphoreType.DMA,
            pltpu.SemaphoreType.DMA,
        ],
        compiler_params=pltpu.CompilerParams(collective_id=0, has_side_effects=True),
    )(amplitudes, ladder_ints, live_count)
    return jnp.transpose(out, (1, 0, 2))


def solution(mesh):
    in_specs = (P("pair", None, "red"), P("pair", "red", None), P())
    out_specs = P("pair", None, "red")
    return jax.shard_map(body, mesh=mesh, in_specs=in_specs, out_specs=out_specs, check_vma=False)
```

time: 51.1 us -> 43.8 us (0.86)
  Pallas kernels: 49.2 us -> 42.1 us
    pallas_call x1, Pallas kernels: 49.2 us -> 42.1 us  [body(): pl.pallas_call(kernel, out_shape=jax.ShapeDtypeStruct((NZ * NX, 2, 256),...]
where the time goes in v2:
time: 43.8 us; the launch traced here: 43.7 us
  Pallas kernels  42.1 us (96%)
  local copies, waits for them, and re-layouts  1.57 us (4%)
    pallas_call x1, Pallas kernels, body(): pl.pallas_call(kernel, out_shape=jax.ShapeDtypeStruct((NZ * NX, 2, 256),...  42.1 us
    transpose x1, local copies, waits for them, and re-layouts, body(): return jnp.transpose(out, (1, 0, 2))  1.57 us

profile of v2, /device:TPU:1, one launch (start us, length us, event | category | flops | bytes accessed | tf_op | source)
XLA Modules:
  0.0 43.7 jit_solution(17772970651474641063)
XLA Ops:
  0.0 42.1 %shard_map.37 = bf16[128,2,256]{2,1,0:T(2,128)(2,1)} custom-call(bf16[2,128,256]{2,1,0:T(8,128)(2,1)} %amp_ref.1, bf16[1,256,1024]{2,1,0:T(8,128)(2,1)} %w_ref.1, s32[128]{0:T(128)} %live_ref.1), custom_call_target="tpu_custom_call" | custom-call | tf_op jit(solution)/shard_map/pallas_call | solution.py:104
  42.1 1.6 %copy.4 = bf16[2,128,256]{2,1,0:T(8,128)(2,1)} copy(bf16[2,128,256]{2,0,1:T(2,128)(2,1)} %bitcast.1) | data formatting | bytes 262144 | tf_op jit(solution)/shard_map/transpose | solution.py:128

commit v3 on v2

v3 whole, which is shorter than its diff:
```python
import jax
import jax.numpy as jnp
from jax import lax
from jax.experimental import pallas as pl
from jax.experimental.pallas import tpu as pltpu
from jax.sharding import PartitionSpec as P

MESH = pl.DeviceIdType.MESH
NZ = 16
NX = 8
NR = 4
LAG = 4
SENDS = [8, 7, 9, 6, 10, 5, 11, 4, 12, 3, 13, 2, 14, 1, 15, 0]
MINE = SENDS.index(0) * NX
GROUPS = [(0,), (1,), (2,), (3,), (4, 5), (6, 7), (15, 14), (13, 12), (8, 9), (10, 11)]


def kernel(amp_ref, w_ref, live_ref, out_ref, amp, w, live, xs, rb, pb, rr, ob,
           lsem, bsem, rsem, osem, bsend, rsend, osend):
    me = lax.axis_index("pair")
    r = lax.axis_index("red")
    z = me // NX
    xc = lax.rem(me, NX)

    partners = []
    for dz in SENDS:
        for k in range(NX):
            if (dz, k) != (0, 0):
                partners.append(lax.rem(z + dz, NZ) * NX + lax.rem(xc + k, NX))

    loads = [pltpu.make_async_copy(amp_ref, amp, lsem.at[0]),
             pltpu.make_async_copy(w_ref, w, lsem.at[1]),
             pltpu.make_async_copy(live_ref, live, lsem.at[2])]
    for copy in loads:
        copy.start()

    barrier = pltpu.get_barrier_semaphore()
    for dz in range(1, NX):
        pl.semaphore_signal(barrier, inc=1, device_id=(z * NX + lax.rem(xc + dz, NX), r), device_id_type=MESH)
    for i in range(NZ - 1):
        zz = i + jnp.where(i >= z, 1, 0)
        for k in range(NX):
            pl.semaphore_signal(barrier, inc=1, device_id=(zz * NX + lax.rem(xc + k, NX), r), device_id_type=MESH)
    for k in range(1, NR):
        pl.semaphore_signal(barrier, inc=1, device_id=(me, lax.rem(r + k, NR)), device_id_type=MESH)

    loads[0].wait()
    xs[...] = jnp.stack([amp[0], amp[1]], axis=1)

    pl.semaphore_wait(barrier, NZ * NX - 1 + NR - 1)
    for p in partners:
        if p is partners[MINE]:
            pltpu.make_async_copy(xs.at[me], rb.at[me], bsem.at[z]).start()
        pltpu.make_async_remote_copy(xs.at[p], rb.at[me], bsend, bsem.at[z],
                                     device_id=(p, r), device_id_type=MESH).start()

    loads[1].wait()
    loads[2].wait()
    limit = live[me] - r * 256
    rows = lax.broadcasted_iota(jnp.int32, (256, 1024), 0)
    w[0] = jnp.where(rows < limit, w[0], jnp.zeros_like(w[0]))

    def multiply(g):
        parts = []
        for zz in GROUPS[g]:
            span = pl.ds(zz * NX, NX)
            pltpu.make_async_copy(rb.at[span], rb.at[span], bsem.at[zz]).wait()
            parts.append(rb[span].reshape(NX * 2, 256))
        rows = jnp.concatenate(parts, axis=0) if len(parts) > 1 else parts[0]
        height = pl.ds(0, rows.shape[0])
        part = jnp.dot(rows, w[0], preferred_element_type=jnp.float32).astype(jnp.bfloat16)
        for j in range(NR):
            pb[g, j, height] = part[:, j * 256:(j + 1) * 256]
        for k in (2, 1, 3):
            rk = lax.rem(r + k, NR)
            pltpu.make_async_remote_copy(pb.at[g, rk, height], rr.at[g, k - 1, height], rsend.at[g], rsem.at[g],
                                         device_id=(me, rk), device_id_type=MESH).start()

    def reduce(g):
        height = pl.ds(0, len(GROUPS[g]) * NX * 2)
        landed = rr.at[g, :, height]
        pltpu.make_async_copy(landed, landed, rsem.at[g]).wait()
        total = pb[g, r, height].astype(jnp.float32)
        for k in range(NR - 1):
            total = total + rr[g, k, height].astype(jnp.float32)
        total = total.astype(jnp.bfloat16)
        for i, zz in enumerate(GROUPS[g]):
            ob[pl.ds(zz * NX, NX)] = total[i * NX * 2:(i + 1) * NX * 2].reshape(NX, 2, 256)
        for zz in GROUPS[g]:
            @pl.when(zz == z)
            def _():
                pltpu.make_async_copy(ob.at[me], out_ref.at[me], osem).start()

            @pl.when(zz != z)
            def _():
                pltpu.make_async_remote_copy(ob.at[zz * NX + xc], out_ref.at[me], osend, osem,
                                             device_id=(zz * NX + xc, r), device_id_type=MESH).start()

            for k in range(1, NX):
                p = zz * NX + lax.rem(xc + k, NX)
                pltpu.make_async_remote_copy(ob.at[p], out_ref.at[me], osend, osem,
                                             device_id=(p, r), device_id_type=MESH).start()

    for t in range(len(GROUPS) + LAG):
        if t < len(GROUPS):
            multiply(t)
        if t >= LAG:
            reduce(t - LAG)

    pltpu.make_async_copy(out_ref, out_ref, osem).wait()
    pltpu.make_async_copy(xs.at[pl.ds(0, NZ * NX - 1)], xs.at[pl.ds(0, NZ * NX - 1)], bsend).wait()
    for g in range(len(GROUPS)):
        sent = rr.at[g, :, pl.ds(0, len(GROUPS[g]) * NX * 2)]
        pltpu.make_async_copy(sent, sent, rsend.at[g]).wait()
    pltpu.make_async_copy(ob.at[pl.ds(0, NZ * NX - 1)], ob.at[pl.ds(0, NZ * NX - 1)], osend).wait()


def body(amplitudes, ladder_ints, live_count):
    any_space = pl.BlockSpec(memory_space=pl.ANY)
    amplitudes, ladder_ints, live_count = [pltpu.with_memory_space_constraint(v, pltpu.HBM) for v in (amplitudes, ladder_ints, live_count)]
    bf16 = jnp.bfloat16
    out = pl.pallas_call(
        kernel,
        out_shape=jax.ShapeDtypeStruct((NZ * NX, 2, 256), bf16),
        in_specs=[pl.BlockSpec(memory_space=pltpu.HBM)] * 3,
        out_specs=any_space,
        scratch_shapes=[
            pltpu.VMEM((2, 128, 256), bf16),
            pltpu.VMEM((1, 256, 1024), bf16),
            pltpu.SMEM((128,), jnp.int32),
            pltpu.VMEM((NZ * NX, 2, 256), bf16),
            pltpu.VMEM((NZ * NX, 2, 256), bf16),
            pltpu.VMEM((len(GROUPS), NR, NX * 4, 256), bf16),
            pltpu.VMEM((len(GROUPS), NR - 1, NX * 4, 256), bf16),
            pltpu.VMEM((NZ * NX, 2, 256), bf16),
            pltpu.SemaphoreType.DMA((3,)),
            pltpu.SemaphoreType.DMA((NZ,)),
            pltpu.SemaphoreType.DMA((len(GROUPS),)),
            pltpu.SemaphoreType.DMA,
            pltpu.SemaphoreType.DMA,
            pltpu.SemaphoreType.DMA((len(GROUPS),)),
            pltpu.SemaphoreType.DMA,
        ],
        compiler_params=pltpu.CompilerParams(collective_id=0, has_side_effects=True, vmem_limit_bytes=8 << 20),
    )(amplitudes, ladder_ints, live_count)
    return jnp.transpose(out, (1, 0, 2))


def solution(mesh):
    in_specs = (P("pair", None, "red"), P("pair", "red", None), P())
    out_specs = P("pair", None, "red")
    return jax.shard_map(body, mesh=mesh, in_specs=in_specs, out_specs=out_specs, check_vma=False)
```

time: 43.8 us -> 41.6 us (0.950)
  Pallas kernels: 42.1 us -> 40.8 us
  local copies, waits for them, and re-layouts: 1.57 us -> 0.67 us
    pallas_call x1, Pallas kernels: 42.1 us -> 40.8 us  [body(): pl.pallas_call(kernel, out_shape=jax.ShapeDtypeStruct((NZ * NX, 2, 256),...]
    transpose x1, local copies, waits for them, and re-layouts: 1.57 us -> 0.67 us  [body(): return jnp.transpose(out, (1, 0, 2))]
where the time goes in v3:
time: 41.6 us; the launch traced here: 41.5 us
  Pallas kernels  40.8 us (98%)
  local copies, waits for them, and re-layouts  0.67 us (2%)
    pallas_call x1, Pallas kernels, body(): pl.pallas_call(kernel, out_shape=jax.ShapeDtypeStruct((NZ * NX, 2, 256),...  40.8 us

profile of v3, /device:TPU:1, one launch (start us, length us, event | category | flops | bytes accessed | tf_op | source)
XLA Modules:
  0.0 41.5 jit_solution(16381252050904812429)
XLA Ops:
  0.0 40.8 %shard_map.37 = bf16[128,2,256]{2,1,0:T(2,128)(2,1)S(1)} custom-call(bf16[2,128,256]{2,1,0:T(8,128)(2,1)} %amp_ref.1, bf16[1,256,1024]{2,1,0:T(8,128)(2,1)} %w_ref.1, s32[128]{0:T(128)} %live_ref.1), custom_call_target="tpu_custom_call" | custom-call | tf_op jit(solution)/shard_map/pallas_call | solution.py:122
  40.8 0.7 %copy.4 = bf16[2,128,256]{2,1,0:T(8,128)(2,1)} copy(bf16[2,128,256]{2,0,1:T(2,128)(2,1)S(1)} %bitcast.1) | data formatting | bytes 262144 | tf_op jit(solution)/shard_map/transpose | solution.py:146

commit v4 on v3

--- a/solution.py
+++ b/solution.py
@@ -11,22 +11,19 @@
 NR = 4
 LAG = 4
 SENDS = [8, 7, 9, 6, 10, 5, 11, 4, 12, 3, 13, 2, 14, 1, 15, 0]
-MINE = SENDS.index(0) * NX
 GROUPS = [(0,), (1,), (2,), (3,), (4, 5), (6, 7), (15, 14), (13, 12), (8, 9), (10, 11)]
 
 
-def kernel(amp_ref, w_ref, live_ref, out_ref, amp, w, live, xs, rb, pb, rr, ob,
-           lsem, bsem, rsem, osem, bsend, rsend, osend):
+def kernel(amp_ref, w_ref, live_ref, out_ref, amp, w, live, xs, pre, rb, pb, rr, ob,
+           plane, column, ready, psem, psend, lsem, bsem, rsem, osem, bsend, rsend, osend):
     me = lax.axis_index("pair")
     r = lax.axis_index("red")
     z = me // NX
     xc = lax.rem(me, NX)
 
-    partners = []
-    for dz in SENDS:
-        for k in range(NX):
-            if (dz, k) != (0, 0):
-                partners.append(lax.rem(z + dz, NZ) * NX + lax.rem(xc + k, NX))
+    core = lax.rem(xc, 2)
+    chip = xc - core
+    twin = me + 1 - 2 * core
 
     loads = [pltpu.make_async_copy(amp_ref, amp, lsem.at[0]),
              pltpu.make_async_copy(w_ref, w, lsem.at[1]),
@@ -35,24 +32,59 @@
         copy.start()
 
     barrier = pltpu.get_barrier_semaphore()
-    for dz in range(1, NX):
-        pl.semaphore_signal(barrier, inc=1, device_id=(z * NX + lax.rem(xc + dz, NX), r), device_id_type=MESH)
+    for k in range(1, NX // 2):
+        pl.semaphore_signal(barrier, inc=1, device_id=(z * NX + lax.rem(chip + 2 * k, NX), r), device_id_type=MESH)
+    for k in range(1, NR):
+        pl.semaphore_signal(barrier, inc=1, device_id=(z * NX + chip, lax.rem(r + k, NR)), device_id_type=MESH)
     for i in range(NZ - 1):
         zz = i + jnp.where(i >= z, 1, 0)
-        for k in range(NX):
-            pl.semaphore_signal(barrier, inc=1, device_id=(zz * NX + lax.rem(xc + k, NX), r), device_id_type=MESH)
-    for k in range(1, NR):
-        pl.semaphore_signal(barrier, inc=1, device_id=(me, lax.rem(r + k, NR)), device_id_type=MESH)
+        pl.semaphore_signal(barrier, inc=1, device_id=(zz * NX + chip + 1, r), device_id_type=MESH)
+
+    @pl.when(core == 1)
+    def _():
+        pl.semaphore_signal(barrier, inc=1, device_id=(twin, r), device_id_type=MESH)
 
     loads[0].wait()
-    xs[...] = jnp.stack([amp[0], amp[1]], axis=1)
+    xs[...] = jnp.stack([amp[0], amp[1]], axis=1).reshape(NZ, NX, 2, 256)
 
-    pl.semaphore_wait(barrier, NZ * NX - 1 + NR - 1)
-    for p in partners:
-        if p is partners[MINE]:
-            pltpu.make_async_copy(xs.at[me], rb.at[me], bsem.at[z]).start()
-        pltpu.make_async_remote_copy(xs.at[p], rb.at[me], bsend, bsem.at[z],
-                                     device_id=(p, r), device_id_type=MESH).start()
+    @pl.when(core == 0)
+    def _():
+        pl.semaphore_wait(barrier, NX - 1 + 2 * (NR - 1))
+        pl.semaphore_signal(plane, inc=1, device_id=(twin, r), device_id_type=MESH)
+
+    @pl.when(core == 1)
+    def _():
+        pl.semaphore_wait(plane, 1)
+
+    for k in range(1, NX):
+        q = lax.rem(xc + k, NX)
+        pltpu.make_async_remote_copy(xs.at[:, q], pre.at[:, xc], psend, psem,
+                                     device_id=(z * NX + q, r), device_id_type=MESH).start()
+    pltpu.make_async_copy(xs.at[:, xc], pre.at[:, xc], psem).start()
+
+    @pl.when(core == 1)
+    def _():
+        pl.semaphore_wait(barrier, 2 * (NZ - 1))
+        pl.semaphore_signal(column, inc=1, device_id=(twin, r), device_id_type=MESH)
+        for k in range(1, NX):
+            if k % 2 == 0:
+                for j in (k, k - 1):
+                    pl.semaphore_signal(ready, inc=1, device_id=(z * NX + lax.rem(xc + j, NX), r), device_id_type=MESH)
+
+    pltpu.make_async_copy(pre, pre, psem).wait()
+
+    @pl.when(core == 0)
+    def _():
+        pl.semaphore_wait(column, 1)
+
+    for dz in SENDS:
+        zz = lax.rem(z + dz, NZ)
+        span = pl.ds(z * NX, NX)
+        if dz:
+            pltpu.make_async_remote_copy(pre.at[zz], rb.at[span], bsend, bsem.at[z],
+                                         device_id=(zz * NX + xc, r), device_id_type=MESH).start()
+        else:
+            pltpu.make_async_copy(pre.at[zz], rb.at[span], bsem.at[z]).start()
 
     loads[1].wait()
     loads[2].wait()
@@ -104,11 +136,14 @@
     for t in range(len(GROUPS) + LAG):
         if t < len(GROUPS):
             multiply(t)
+        if t == LAG:
+            pl.semaphore_wait(ready, NX // 2 - 1)
         if t >= LAG:
             reduce(t - LAG)
 
     pltpu.make_async_copy(out_ref, out_ref, osem).wait()
-    pltpu.make_async_copy(xs.at[pl.ds(0, NZ * NX - 1)], xs.at[pl.ds(0, NZ * NX - 1)], bsend).wait()
+    pltpu.make_async_copy(xs.at[:, pl.ds(0, NX - 1)], xs.at[:, pl.ds(0, NX - 1)], psend).wait()
+    pltpu.make_async_copy(pre.at[pl.ds(0, NZ - 1)], pre.at[pl.ds(0, NZ - 1)], bsend).wait()
     for g in range(len(GROUPS)):
         sent = rr.at[g, :, pl.ds(0, len(GROUPS[g]) * NX * 2)]
         pltpu.make_async_copy(sent, sent, rsend.at[g]).wait()
@@ -128,11 +163,17 @@
             pltpu.VMEM((2, 128, 256), bf16),
             pltpu.VMEM((1, 256, 1024), bf16),
             pltpu.SMEM((128,), jnp.int32),
-            pltpu.VMEM((NZ * NX, 2, 256), bf16),
+            pltpu.VMEM((NZ, NX, 2, 256), bf16),
+            pltpu.VMEM((NZ, NX, 2, 256), bf16),
             pltpu.VMEM((NZ * NX, 2, 256), bf16),
             pltpu.VMEM((len(GROUPS), NR, NX * 4, 256), bf16),
             pltpu.VMEM((len(GROUPS), NR - 1, NX * 4, 256), bf16),
             pltpu.VMEM((NZ * NX, 2, 256), bf16),
+            pltpu.SemaphoreType.REGULAR,
+            pltpu.SemaphoreType.REGULAR,
+            pltpu.SemaphoreType.REGULAR,
+            pltpu.SemaphoreType.DMA,
+            pltpu.SemaphoreType.DMA,
             pltpu.SemaphoreType.DMA((3,)),
             pltpu.SemaphoreType.DMA((NZ,)),
             pltpu.SemaphoreType.DMA((len(GROUPS),)),

time: 41.6 us -> 39.4 us (0.947)
  Pallas kernels: 40.8 us -> 38.6 us
    pallas_call x1, Pallas kernels: 40.8 us -> 38.6 us  [body(): pl.pallas_call(kernel, out_shape=jax.ShapeDtypeStruct((NZ * NX, 2, 256),...]
where the time goes in v4:
time: 39.4 us; the launch traced here: 39.3 us
  Pallas kernels  38.6 us (98%)
  local copies, waits for them, and re-layouts  0.67 us (2%)
    pallas_call x1, Pallas kernels, body(): pl.pallas_call(kernel, out_shape=jax.ShapeDtypeStruct((NZ * NX, 2, 256),...  38.6 us

profile of v4, /device:TPU:1, one launch (start us, length us, event | category | flops | bytes accessed | tf_op | source)
XLA Modules:
  0.0 39.3 jit_solution(9684284049697001410)
XLA Ops:
  0.0 38.6 %shard_map.37 = bf16[128,2,256]{2,1,0:T(2,128)(2,1)S(1)} custom-call(bf16[2,128,256]{2,1,0:T(8,128)(2,1)} %amp_ref.1, bf16[1,256,1024]{2,1,0:T(8,128)(2,1)} %w_ref.1, s32[128]{0:T(128)} %live_ref.1), custom_call_target="tpu_custom_call" | custom-call | tf_op jit(solution)/shard_map/pallas_call | solution.py:157
  38.6 0.7 %copy.4 = bf16[2,128,256]{2,1,0:T(8,128)(2,1)} copy(bf16[2,128,256]{2,0,1:T(2,128)(2,1)S(1)} %bitcast.1) | data formatting | bytes 262144 | tf_op jit(solution)/shard_map/transpose | solution.py:187

commit v5 on v4

--- a/solution.py
+++ b/solution.py
@@ -9,7 +9,7 @@
 NZ = 16
 NX = 8
 NR = 4
-LAG = 4
+LAG = 5
 SENDS = [8, 7, 9, 6, 10, 5, 11, 4, 12, 3, 13, 2, 14, 1, 15, 0]
 GROUPS = [(0,), (1,), (2,), (3,), (4, 5), (6, 7), (15, 14), (13, 12), (8, 9), (10, 11)]
 
@@ -25,25 +25,30 @@
     chip = xc - core
     twin = me + 1 - 2 * core
 
+    barrier = pltpu.get_barrier_semaphore()
+
+    def greet(count, first):
+        for i in range(first, first + count):
+            zz = i + jnp.where(i >= z, 1, 0)
+            pl.semaphore_signal(barrier, inc=1, device_id=(zz * NX + chip + 1, r), device_id_type=MESH)
+
+    greet(4, 0)
     loads = [pltpu.make_async_copy(amp_ref, amp, lsem.at[0]),
              pltpu.make_async_copy(w_ref, w, lsem.at[1]),
              pltpu.make_async_copy(live_ref, live, lsem.at[2])]
-    for copy in loads:
-        copy.start()
-
-    barrier = pltpu.get_barrier_semaphore()
+    loads[0].start()
     for k in range(1, NX // 2):
         pl.semaphore_signal(barrier, inc=1, device_id=(z * NX + lax.rem(chip + 2 * k, NX), r), device_id_type=MESH)
     for k in range(1, NR):
         pl.semaphore_signal(barrier, inc=1, device_id=(z * NX + chip, lax.rem(r + k, NR)), device_id_type=MESH)
-    for i in range(NZ - 1):
-        zz = i + jnp.where(i >= z, 1, 0)
-        pl.semaphore_signal(barrier, inc=1, device_id=(zz * NX + chip + 1, r), device_id_type=MESH)
 
     @pl.when(core == 1)
     def _():
         pl.semaphore_signal(barrier, inc=1, device_id=(twin, r), device_id_type=MESH)
 
+    greet(NZ - 5, 4)
+    loads[1].start()
+    loads[2].start()
     loads[0].wait()
     xs[...] = jnp.stack([amp[0], amp[1]], axis=1).reshape(NZ, NX, 2, 256)
 
@@ -61,6 +66,12 @@
         pltpu.make_async_remote_copy(xs.at[:, q], pre.at[:, xc], psend, psem,
                                      device_id=(z * NX + q, r), device_id_type=MESH).start()
     pltpu.make_async_copy(xs.at[:, xc], pre.at[:, xc], psem).start()
+
+    loads[1].wait()
+    loads[2].wait()
+    limit = live[me] - r * 256
+    rows = lax.broadcasted_iota(jnp.int32, (256, 1024), 0)
+    w[0] = jnp.where(rows < limit, w[0], jnp.zeros_like(w[0]))
 
     @pl.when(core == 1)
     def _():
@@ -85,12 +96,6 @@
                                          device_id=(zz * NX + xc, r), device_id_type=MESH).start()
         else:
             pltpu.make_async_copy(pre.at[zz], rb.at[span], bsem.at[z]).start()
-
-    loads[1].wait()
-    loads[2].wait()
-    limit = live[me] - r * 256
-    rows = lax.broadcasted_iota(jnp.int32, (256, 1024), 0)
-    w[0] = jnp.where(rows < limit, w[0], jnp.zeros_like(w[0]))
 
     def multiply(g):
         parts = []
@@ -103,9 +108,10 @@
         part = jnp.dot(rows, w[0], preferred_element_type=jnp.float32).astype(jnp.bfloat16)
         for j in range(NR):
             pb[g, j, height] = part[:, j * 256:(j + 1) * 256]
-        for k in (2, 1, 3):
-            rk = lax.rem(r + k, NR)
-            pltpu.make_async_remote_copy(pb.at[g, rk, height], rr.at[g, k - 1, height], rsend.at[g], rsem.at[g],
+        for i in range(NR - 1):
+            rk = i + jnp.where(i >= r, 1, 0)
+            slot = r - jnp.where(i >= r, 0, 1)
+            pltpu.make_async_remote_copy(pb.at[g, rk, height], rr.at[g, slot, height], rsend.at[g], rsem.at[g],
                                          device_id=(me, rk), device_id_type=MESH).start()
 
     def reduce(g):
@@ -119,6 +125,19 @@
         for i, zz in enumerate(GROUPS[g]):
             ob[pl.ds(zz * NX, NX)] = total[i * NX * 2:(i + 1) * NX * 2].reshape(NX, 2, 256)
         for zz in GROUPS[g]:
+            if zz == 0:
+                for p in (1, 0, 2, 3, 6, 7, 4, 5):
+                    @pl.when(p != me)
+                    def _():
+                        pltpu.make_async_remote_copy(ob.at[p], out_ref.at[me], osend, osem,
+                                                     device_id=(p, r), device_id_type=MESH).start()
+
+                    @pl.when(p == me)
+                    def _():
+                        pltpu.make_async_copy(ob.at[p], out_ref.at[me], osem).start()
+
+                continue
+
             @pl.when(zz == z)
             def _():
                 pltpu.make_async_copy(ob.at[me], out_ref.at[me], osem).start()

time: 39.4 us -> 39 us (0.990)
  Pallas kernels: 38.6 us -> 38.2 us
    pallas_call x1, Pallas kernels: 38.6 us -> 38.2 us  [body(): pl.pallas_call(kernel, out_shape=jax.ShapeDtypeStruct((NZ * NX, 2, 256),...]
where the time goes in v5:
time: 39 us; the launch traced here: 38.9 us
  Pallas kernels  38.2 us (98%)
  local copies, waits for them, and re-layouts  0.67 us (2%)
    pallas_call x1, Pallas kernels, body(): pl.pallas_call(kernel, out_shape=jax.ShapeDtypeStruct((NZ * NX, 2, 256),...  38.2 us

profile of v5, /device:TPU:1, one launch (start us, length us, event | category | flops | bytes accessed | tf_op | source)
XLA Modules:
  0.0 38.9 jit_solution(102535810710057648)
XLA Ops:
  0.0 38.2 %shard_map.37 = bf16[128,2,256]{2,1,0:T(2,128)(2,1)S(1)} custom-call(bf16[2,128,256]{2,1,0:T(8,128)(2,1)} %amp_ref.1, bf16[1,256,1024]{2,1,0:T(8,128)(2,1)} %w_ref.1, s32[128]{0:T(128)} %live_ref.1), custom_call_target="tpu_custom_call" | custom-call | tf_op jit(solution)/shard_map/pallas_call | solution.py:176
  38.2 0.7 %copy.4 = bf16[2,128,256]{2,1,0:T(8,128)(2,1)} copy(bf16[2,128,256]{2,0,1:T(2,128)(2,1)S(1)} %bitcast.1) | data formatting | bytes 262144 | tf_op jit(solution)/shard_map/transpose | solution.py:206

commit v6 on v5

--- a/solution.py
+++ b/solution.py
@@ -11,6 +11,7 @@
 NR = 4
 LAG = 5
 SENDS = [8, 7, 9, 6, 10, 5, 11, 4, 12, 3, 13, 2, 14, 1, 15, 0]
+OTHER = [1, 15, 2, 14, 3, 13, 4, 12, 5, 11, 6, 10, 7, 9, 8, 0]
 GROUPS = [(0,), (1,), (2,), (3,), (4, 5), (6, 7), (15, 14), (13, 12), (8, 9), (10, 11)]
 
 
@@ -88,14 +89,15 @@
     def _():
         pl.semaphore_wait(column, 1)
 
-    for dz in SENDS:
-        zz = lax.rem(z + dz, NZ)
-        span = pl.ds(z * NX, NX)
+    late = z >= NZ // 2
+    span = pl.ds(z * NX, NX)
+    for dz, other in zip(SENDS, OTHER):
+        zz = lax.rem(z + jnp.where(late, jnp.where(core == 0, NZ - other, other), jnp.where(core == 0, NZ - dz, dz)), NZ)
         if dz:
             pltpu.make_async_remote_copy(pre.at[zz], rb.at[span], bsend, bsem.at[z],
                                          device_id=(zz * NX + xc, r), device_id_type=MESH).start()
         else:
-            pltpu.make_async_copy(pre.at[zz], rb.at[span], bsem.at[z]).start()
+            pltpu.make_async_copy(pre.at[z], rb.at[span], bsem.at[z]).start()
 
     def multiply(g):
         parts = []

time: 39 us -> 38.8 us (level)
  no operation moved by 1% of the time
where the time goes in v6:
time: 38.8 us; the launch traced here: 38.7 us
  Pallas kernels  38 us (98%)
  local copies, waits for them, and re-layouts  0.67 us (2%)
    pallas_call x1, Pallas kernels, body(): pl.pallas_call(kernel, out_shape=jax.ShapeDtypeStruct((NZ * NX, 2, 256),...  38 us

profile of v6, /device:TPU:1, one launch (start us, length us, event | category | flops | bytes accessed | tf_op | source)
XLA Modules:
  0.0 38.7 jit_solution(2312550671144742927)
XLA Ops:
  0.0 38.0 %shard_map.37 = bf16[128,2,256]{2,1,0:T(2,128)(2,1)S(1)} custom-call(bf16[2,128,256]{2,1,0:T(8,128)(2,1)} %amp_ref.1, bf16[1,256,1024]{2,1,0:T(8,128)(2,1)} %w_ref.1, s32[128]{0:T(128)} %live_ref.1), custom_call_target="tpu_custom_call" | custom-call | tf_op jit(solution)/shard_map/pallas_call | solution.py:178
  38.0 0.7 %copy.4 = bf16[2,128,256]{2,1,0:T(8,128)(2,1)} copy(bf16[2,128,256]{2,0,1:T(2,128)(2,1)S(1)} %bitcast.1) | data formatting | bytes 262144 | tf_op jit(solution)/shard_map/transpose | solution.py:208

commit v7 on v6

--- a/solution.py
+++ b/solution.py
@@ -162,13 +162,13 @@
         if t >= LAG:
             reduce(t - LAG)
 
-    pltpu.make_async_copy(out_ref, out_ref, osem).wait()
     pltpu.make_async_copy(xs.at[:, pl.ds(0, NX - 1)], xs.at[:, pl.ds(0, NX - 1)], psend).wait()
     pltpu.make_async_copy(pre.at[pl.ds(0, NZ - 1)], pre.at[pl.ds(0, NZ - 1)], bsend).wait()
     for g in range(len(GROUPS)):
         sent = rr.at[g, :, pl.ds(0, len(GROUPS[g]) * NX * 2)]
         pltpu.make_async_copy(sent, sent, rsend.at[g]).wait()
     pltpu.make_async_copy(ob.at[pl.ds(0, NZ * NX - 1)], ob.at[pl.ds(0, NZ * NX - 1)], osend).wait()
+    pltpu.make_async_copy(out_ref, out_ref, osem).wait()
 
 
 def body(amplitudes, ladder_ints, live_count):

time: 38.8 us -> 38.8 us (level)
  no operation moved by 1% of the time
where the time goes in v7:
time: 38.8 us; the launch traced here: 38.7 us
  Pallas kernels  38 us (98%)
  local copies, waits for them, and re-layouts  0.67 us (2%)
    pallas_call x1, Pallas kernels, body(): pl.pallas_call(kernel, out_shape=jax.ShapeDtypeStruct((NZ * NX, 2, 256),...  38 us

profile of v7, /device:TPU:1, one launch (start us, length us, event | category | flops | bytes accessed | tf_op | source)
XLA Modules:
  0.0 38.7 jit_solution(9347073845384156837)
XLA Ops:
  0.0 38.0 %shard_map.37 = bf16[128,2,256]{2,1,0:T(2,128)(2,1)S(1)} custom-call(bf16[2,128,256]{2,1,0:T(8,128)(2,1)} %amp_ref.1, bf16[1,256,1024]{2,1,0:T(8,128)(2,1)} %w_ref.1, s32[128]{0:T(128)} %live_ref.1), custom_call_target="tpu_custom_call" | custom-call | tf_op jit(solution)/shard_map/pallas_call | solution.py:178
  38.0 0.7 %copy.4 = bf16[2,128,256]{2,1,0:T(8,128)(2,1)} copy(bf16[2,128,256]{2,0,1:T(2,128)(2,1)S(1)} %bitcast.1) | data formatting | bytes 262144 | tf_op jit(solution)/shard_map/transpose | solution.py:208

commit v8 on v7

--- a/solution.py
+++ b/solution.py
@@ -78,10 +78,6 @@
     def _():
         pl.semaphore_wait(barrier, 2 * (NZ - 1))
         pl.semaphore_signal(column, inc=1, device_id=(twin, r), device_id_type=MESH)
-        for k in range(1, NX):
-            if k % 2 == 0:
-                for j in (k, k - 1):
-                    pl.semaphore_signal(ready, inc=1, device_id=(z * NX + lax.rem(xc + j, NX), r), device_id_type=MESH)
 
     pltpu.make_async_copy(pre, pre, psem).wait()
 
@@ -98,6 +94,13 @@
                                          device_id=(zz * NX + xc, r), device_id_type=MESH).start()
         else:
             pltpu.make_async_copy(pre.at[z], rb.at[span], bsem.at[z]).start()
+
+    @pl.when(core == 1)
+    def _():
+        for k in range(1, NX):
+            if k % 2 == 0:
+                for j in (k, k - 1):
+                    pl.semaphore_signal(ready, inc=1, device_id=(z * NX + lax.rem(xc + j, NX), r), device_id_type=MESH)
 
     def multiply(g):
         parts = []

time: 38.8 us -> 38.9 us (level)
  no operation moved by 1% of the time
where the time goes in v8:
time: 38.9 us; the launch traced here: 38.8 us
  Pallas kernels  38.1 us (98%)
  local copies, waits for them, and re-layouts  0.67 us (2%)
    pallas_call x1, Pallas kernels, body(): pl.pallas_call(kernel, out_shape=jax.ShapeDtypeStruct((NZ * NX, 2, 256),...  38.1 us

profile of v8, /device:TPU:1, one launch (start us, length us, event | category | flops | bytes accessed | tf_op | source)
XLA Modules:
  0.0 38.8 jit_solution(704965631922159187)
XLA Ops:
  0.0 38.1 %shard_map.37 = bf16[128,2,256]{2,1,0:T(2,128)(2,1)S(1)} custom-call(bf16[2,128,256]{2,1,0:T(8,128)(2,1)} %amp_ref.1, bf16[1,256,1024]{2,1,0:T(8,128)(2,1)} %w_ref.1, s32[128]{0:T(128)} %live_ref.1), custom_call_target="tpu_custom_call" | custom-call | tf_op jit(solution)/shard_map/pallas_call | solution.py:181
  38.1 0.7 %copy.4 = bf16[2,128,256]{2,1,0:T(8,128)(2,1)} copy(bf16[2,128,256]{2,0,1:T(2,128)(2,1)S(1)} %bitcast.1) | data formatting | bytes 262144 | tf_op jit(solution)/shard_map/transpose | solution.py:211
